TPU v7x, 256 devices: a whole 4x4x8 slice. The times are simulated.
256 devices in a mesh: bl: 64 (over y, z, core), ch: 4 (over x).
Axes of the slice: x: 4, y: 4, z: 8, core: 2. Of those that a mesh axis runs over, the one named last changes fastest.
Arguments:
- facet_grid: bfloat16 [4, 64, 16, 1024], P(None, None, None, 'ch'), may hold values from -0.75 to 0.75
- kernel: bfloat16 [131072, 1024], P('bl', 'ch'), may hold values from -0.1875 to 0.1875
- tile_of: int32 [256], P('bl'), may hold values from 0 to 3
- observed: bfloat16 [64, 2, 131072], P('ch', None, 'bl'), may hold values from -6 to 6
- flags: int32 [64, 131072], P('ch', 'bl'), may hold values 0 or 1
- pairs: int32 [2, 131072], P(None, 'bl'), may hold values from 0 to 511, as said below
- solver_order: int32 [512], replicated, may hold values from 0 to 511, as said below
Outputs:
- gains: float32 [64, 16, 512], P('ch', None, 'bl')
Inputs may be any that keep to these rules, and one draw needn't show every extreme that they name: `solver_order`: each station appears once. `pairs`: for row r, with j = (r mod 2048) // 32, the first station is solver_order[8 * j + m] for some m below 8; the second station differs from the first.
All inputs are finite; a program needn't handle non-finite values. No bound on the sum of `flags` on one device may be relied on, other than what follows from the above.
Results may differ from a plain program's by a relative error of at most 0.013.
Values may be sent and summed in bfloat16 or wider, within the bound.
No kernel may reach another device: no remote copies, remote signals or barrier semaphores. Data moves between devices by JAX's collectives and lax.ppermute only.
A program may use at most 128 MiB of HBM per device.

v0:
```python
import jax
import jax.numpy as jnp
from jax import lax
from jax.sharding import PartitionSpec as P

S = 512
ND = 8
ITERS = 4


def extended(shard, sides, width):
    for axis, dim in sides:
        devices, length = (lax.axis_size(axis), shard.shape[dim])
        up = [(i, (i + 1) % devices) for i in range(devices - 1)]
        down = [(j, i) for i, j in up]
        last = lax.slice_in_dim(shard, length - width, length, axis=dim)
        initial = lax.slice_in_dim(shard, 0, width, axis=dim)
        before = lax.ppermute(last, axis, up)
        after = lax.ppermute(initial, axis, down)
        shard = jnp.concatenate([before, shard, after], axis=dim)
    return shard


def lookup(gain_flat, pick):
    return jnp.dot(
        gain_flat, pick, precision=lax.Precision.HIGHEST, preferred_element_type=jnp.float32
    )


def row_terms(model_vis, visible, far_gain, near_gain):
    channels = model_vis.shape[0]
    row_count = model_vis.shape[2]
    model_pair = model_vis.reshape(channels, ND, 2, row_count)
    model_re = model_pair[:, :, 0].astype(jnp.float32)
    model_im = model_pair[:, :, 1].astype(jnp.float32)
    far_pair = far_gain.reshape(channels, ND, 2, row_count)
    near_pair = near_gain.reshape(channels, ND, 2, row_count)
    far_re = far_pair[:, :, 0]
    far_im = far_pair[:, :, 1]
    near_re = near_pair[:, :, 0]
    near_im = near_pair[:, :, 1]
    prod_re = model_re * far_re + model_im * far_im
    prod_im = model_im * far_re - model_re * far_im
    pred_re = jnp.sum(near_re * prod_re - near_im * prod_im, axis=1)
    pred_im = jnp.sum(near_re * prod_im + near_im * prod_re, axis=1)
    resid_re = visible[:, 0].astype(jnp.float32) - pred_re
    resid_im = visible[:, 1].astype(jnp.float32) - pred_im
    cross_re = prod_re * resid_re[:, None, :] + prod_im * resid_im[:, None, :]
    cross_im = prod_re * resid_im[:, None, :] - prod_im * resid_re[:, None, :]
    power = prod_re * prod_re + prod_im * prod_im
    stacked = jnp.concatenate([cross_re, cross_im, power], axis=1)
    return stacked.reshape(channels * 3 * ND, row_count)


def update_gains(gain_shard, sum_re, sum_im, power):
    channels = gain_shard.shape[0]
    owned = gain_shard.shape[2]
    gain_pair = gain_shard.reshape(channels, ND, 2, owned)
    gain_re = gain_pair[:, :, 0]
    gain_im = gain_pair[:, :, 1]
    new_re = (sum_re + gain_re * power) / (power + 1.0)
    new_im = (sum_im + gain_im * power) / (power + 1.0)
    averaged = jnp.stack([(gain_re + new_re) * 0.5, (gain_im + new_im) * 0.5], axis=2).reshape(
        channels, 2 * ND, owned
    )
    padded = extended(averaged, (("ch", 0),), 1)
    total_channels = channels * lax.axis_size("ch")
    chan_index = lax.axis_index("ch") * channels + jnp.arange(channels, dtype=jnp.int32)
    has_left = (chan_index > 0).astype(jnp.float32)[:, None, None]
    has_right = (chan_index < total_channels - 1).astype(jnp.float32)[:, None, None]
    return (0.25 * has_left * padded[:-2] + 0.5 * padded[1:-1] + 0.25 * has_right * padded[2:]) / (
        0.5 + 0.25 * has_left + 0.25 * has_right
    )


def body(facet_grid, kernel, tile_of, observed, flags, pairs, solver_order):
    channels = observed.shape[0]
    row_count = observed.shape[2]
    cell_count = kernel.shape[1]
    tile_count = facet_grid.shape[0]
    block_count = tile_of.shape[0]
    block_rows = row_count // block_count
    tile_pick = (tile_of[:, None] == jnp.arange(tile_count, dtype=jnp.int32)[None, :]).astype(
        jnp.bfloat16
    )
    kernel_blocks = kernel.reshape(block_count, block_rows, cell_count)
    chosen = jnp.einsum(
        "bt,tckg->bckg", tile_pick, facet_grid, preferred_element_type=jnp.float32
    ).astype(jnp.bfloat16)
    partial_vis = jnp.einsum(
        "bckg,bvg->ckbv", chosen, kernel_blocks, preferred_element_type=jnp.float32
    )
    summed = lax.psum_scatter(
        partial_vis.reshape(channels * lax.axis_size("ch"), partial_vis.shape[1], row_count).astype(
            jnp.bfloat16
        ),
        "ch",
        scatter_dimension=0,
        tiled=True,
    ).astype(jnp.float32)
    kept_rows = (1 - flags).astype(jnp.float32)
    model_vis = (summed * kept_rows[:, None, :]).astype(jnp.bfloat16)
    visible = (observed.astype(jnp.float32) * kept_rows[:, None, :]).astype(jnp.bfloat16)
    inverse = jnp.zeros((S,), jnp.int32).at[solver_order].set(jnp.arange(S, dtype=jnp.int32))
    bl_count = lax.axis_size("bl")
    owned = S // bl_count
    station_ids = jnp.arange(S, dtype=jnp.int32)[:, None]
    packed = pairs.reshape(1, 2, row_count)
    model_vis, visible, packed = (
        lax.all_to_all(model_vis, "bl", split_axis=2, concat_axis=2, tiled=True),
        lax.all_to_all(visible, "bl", split_axis=2, concat_axis=2, tiled=True),
        lax.all_to_all(packed, "bl", split_axis=2, concat_axis=2, tiled=True),
    )
    first_slot = inverse[packed[0, 0]]
    second_slot = inverse[packed[0, 1]]
    owner_slot = first_slot - lax.axis_index("bl") * owned
    near_pick = (owner_slot[None, :] == jnp.arange(owned, dtype=jnp.int32)[:, None]).astype(
        jnp.float32
    )
    far_pick = (second_slot[None, :] == station_ids).astype(jnp.float32)
    gain_shard = (
        jnp.zeros((channels, ND, 2, owned), jnp.float32)
        .at[:, :, 0, :]
        .set(1.0)
        .reshape(channels, 2 * ND, owned)
    )
    all_gains = (
        jnp.zeros((channels, ND, 2, S), jnp.float32)
        .at[:, :, 0, :]
        .set(1.0)
        .reshape(channels, 2 * ND, S)
    )
    for iteration in range(ITERS):
        if iteration > 0:
            all_gains = lax.all_gather(gain_shard, "bl", axis=2, tiled=True)
        far_gain = lookup(all_gains.reshape(channels * 2 * ND, S), far_pick)
        near_gain = lookup(gain_shard.reshape(channels * 2 * ND, owned), near_pick)
        stacked = row_terms(model_vis, visible, far_gain, near_gain)
        station_terms = jnp.einsum(
            "fv,sv->fs",
            stacked,
            near_pick,
            precision=lax.Precision.HIGHEST,
            preferred_element_type=jnp.float32,
        )
        mine = station_terms.reshape(channels, 3 * ND, owned)
        sum_re = mine[:, :ND]
        sum_im = mine[:, ND : 2 * ND]
        sum_power = mine[:, 2 * ND :]
        gain_shard = update_gains(gain_shard, sum_re, sum_im, sum_power)
    return gain_shard


def solution(mesh):
    in_specs = (
        P(None, None, None, "ch"),
        P("bl", "ch"),
        P("bl"),
        P("ch", None, "bl"),
        P("ch", "bl"),
        P(None, "bl"),
        P(),
    )
    out_specs = P("ch", None, "bl")
    return jax.shard_map(body, mesh=mesh, in_specs=in_specs, out_specs=out_specs, check_vma=False)
```

profile of v0, /device:TPU:1, one launch (start us, length us, event | category | flops | bytes accessed | tf_op | source)
XLA Modules:
  0.0 517.9 jit_solution(18245494994774000052)
XLA Ops:
  6.5 1.6 copy-done
  8.1 2.4 fusion.41
  11.9 2.6 copy.212
  16.5 13.1 %all-to-all-start.1 = ((s32[1,2,2048]{1,0,2:T(1,128)}), s32[1,2,2048]{1,0,2:T(1,128)S(1)}, u32[]{:S(2)}, u32[]{:S(2)}) async-start(s32[1,2,2048]{1,0,2:T(1,128)} %bitcast.7), calls=%async_computation.2 | async-start | bytes 2097152 | tf_op jit(solution)/shard_map/all_to_all | solution.py:112
  30.7 1.8 reshape.311
  32.5 2.4 scatter_custom_fusion
  35.0 23.2 %all-to-all-done.1 = s32[1,2,2048]{1,0,2:T(1,128)S(1)} async-done(((s32[1,2,2048]{1,0,2:T(1,128)}), s32[1,2,2048]{1,0,2:T(1,128)S(1)}, u32[]{:S(2)}, u32[]{:S(2)}) %all-to-all-start.1) | async-done | bytes 16416 | tf_op jit(solution)/shard_map/all_to_all | solution.py:112
  58.2 6.2 %all-to-all-start.2 = ((bf16[64,2,512]{2,1,0:T(2,128)(2,1)}), bf16[64,2,512]{2,1,0:T(2,128)(2,1)S(1)}, u32[]{:S(2)}, u32[]{:S(2)}) async-start(bf16[64,2,512]{2,1,0:T(2,128)(2,1)} %reshape.311), calls=%async_computation.3 | async-start | bytes 262144 | tf_op jit(solution)/shard_map/all_to_all | solution.py:111
  64.4 106.4 %slice_reduce_fusion = (s32[2048]{0:T(1024)S(1)}, s32[2048]{0:T(1024)S(1)}) fusion(s32[1,2,2048]{1,0,2:T(1,128)S(1)} %all-to-all-done.1), kind=kLoop, calls=%fused_computation.86 | loop fusion | bytes 32768 | tf_op jit(solution)/shard_map/slice | solution.py:114
  170.9 1.5 multiply_convert_fusion
  172.4 8.6 %copy.107 = bf16[16,16,2048]{1,0,2:T(8,128)(2,1)} copy(bf16[16,16,2048]{2,1,0:T(8,128)(2,1)S(1)} %multiply_convert_fusion) | data formatting | bytes 2097152 | tf_op jit(solution)/shard_map/convert_element_type | solution.py:102
  181.0 12.5 %reshape.309 = bf16[64,2,4096]{2,1,0:T(2,128)(2,1)} reshape(bf16[2048,16,16]{2,1,0:T(8,128)(2,1)} %bitcast.247) | data formatting | bytes 2097152
  193.4 10.7 %all-to-all-start = ((bf16[64,2,4096]{2,1,0:T(2,128)(2,1)}), bf16[64,2,4096]{2,1,0:T(2,128)(2,1)S(1)}, u32[]{:S(2)}, u32[]{:S(2)}) async-start(bf16[64,2,4096]{2,1,0:T(2,128)(2,1)} %reshape.309), calls=%async_computation.1 | async-start | bytes 2097152 | tf_op jit(solution)/shard_map/all_to_all | solution.py:110
  204.1 13.2 %gather_fusion.1 = s32[2048]{0:T(1024)S(1)} fusion(s32[512]{0:T(512)S(1)} %scatter_custom_fusion, s32[2048]{0:T(1024)S(1)} %broadcast_clamp_fusion), kind=kCustom, calls=%fused_computation.1 | custom fusion | bytes 24576 | tf_op jit(solution)/shard_map/gather | solution.py:114
  217.4 13.2 %gather_fusion = s32[2048]{0:T(1024)S(1)} fusion(s32[512]{0:T(512)S(1)} %scatter_custom_fusion, s32[2048]{0:T(1024)S(1)} %broadcast_clamp_fusion.1), kind=kCustom, calls=%fused_computation | custom fusion | bytes 24576 | tf_op jit(solution)/shard_map/gather | solution.py:115
  230.7 2.4 fusion.129
  233.0 3.4 fusion.8
  237.1 2.3 fusion.168
  239.4 2.2 copy.203
  242.2 7.6 %reshape.310 = bf16[2048,16,16]{2,1,0:T(8,128)(2,1)} reshape(bf16[64,2,4096]{2,1,0:T(2,128)(2,1)S(1)} %all-to-all-done) | data formatting | bytes 2097152
  249.8 9.1 %copy.108 = bf16[16,16,2048]{2,0,1:T(8,128)(2,1)S(1)} copy(bf16[16,16,2048]{1,0,2:T(8,128)(2,1)} %bitcast.248) | data formatting | bytes 2097152 | tf_op jit(solution)/shard_map/all_to_all | solution.py:110
  259.0 1.5 copy-done.2
  260.5 2.9 subtract_reduce_fusion.3
  264.0 3.9 fusion.10
  269.7 4.0 collective-permute-start
  274.7 56.0 %all_gather.9 = f32[16,16,512]{0,2,1:T(8,128)} all-gather(f32[16,16,8]{0,2,1:T(8,128)S(1)} %fusion.111), channel_id=1, replica_groups=mesh['bl'=64,'ch'=4] {'bl'}, dimensions={2}, use_global_device_ids=true | all-gather | bytes 532480 | tf_op jit(solution)/shard_map/all_gather | solution.py:135
  331.5 2.9 copy.176
  334.4 2.1 fusion.4
  338.9 1.5 copy.205
  340.4 1.5 copy.206
  342.3 3.9 fusion.16
  346.7 3.6 collective-permute-start.2
  352.0 3.6 collective-permute-done.3
  355.7 53.5 %all_gather.10 = f32[16,16,512]{0,2,1:T(8,128)} all-gather(f32[16,16,8]{0,2,1:T(8,128)S(1)} %fusion.98), channel_id=1, replica_groups=mesh['bl'=64,'ch'=4] {'bl'}, dimensions={2}, use_global_device_ids=true | all-gather | bytes 532480 | tf_op jit(solution)/shard_map/all_gather | solution.py:135
  410.0 2.9 copy.180
  412.9 2.1 fusion.2
  418.8 1.5 copy.208
  420.8 3.9 fusion.22
  425.1 3.1 collective-permute-start.4
  430.0 3.6 collective-permute-done.5
  433.6 53.5 %all_gather.11 = f32[16,16,512]{0,2,1:T(8,128)} all-gather(f32[16,16,8]{0,2,1:T(8,128)S(1)} %fusion.85), channel_id=1, replica_groups=mesh['bl'=64,'ch'=4] {'bl'}, dimensions={2}, use_global_device_ids=true | all-gather | bytes 532480 | tf_op jit(solution)/shard_map/all_gather | solution.py:135
  487.2 2.9 copy.184
  490.1 2.1 fusion.6
  493.2 1.9 subtract_reduce_fusion
  495.4 1.8 multiply_add_fusion.1
  497.2 3.9 fusion.28
  501.6 3.1 collective-permute-start.6
  506.4 3.6 collective-permute-done.7
  (132 shorter events, 26.1 us)
Async XLA Ops:
  6.5 1.6 copy-start
  6.5 4.0 copy-start.3
  6.5 164.3 %reduce-scatter.2.cloned.1.call-start = ((), (), s32[]{:S(2)}) async-start(), calls=%async_computation.4 | async-start | bytes 5242880 | tf_op jit(solution)/shard_map/reduce_scatter | solution.py:93
  14.5 0.7 copy-start.11
  14.5 15.2 %copy-start.19 = (s32[512]{0:T(512)S(1)}, s32[512]{0:T(512)}, u32[]{:S(2)}) copy-start(s32[512]{0:T(512)} %param.17) | copy-start | bytes 6148
  14.5 15.3 %copy-start.10 = (s32[16,2048]{1,0:T(8,128)S(1)}, s32[16,2048]{1,0:T(8,128)}, u32[]{:S(2)}) copy-start(s32[16,2048]{1,0:T(8,128)} %param.15) | copy-start | bytes 393220
  14.5 15.3 %copy-start.8 = (bf16[16,2,2048]{2,1,0:T(2,128)(2,1)S(1)}, bf16[16,2,2048]{2,1,0:T(2,128)(2,1)}, u32[]{:S(2)}) copy-start(bf16[16,2,2048]{2,1,0:T(2,128)(2,1)} %param.14) | copy-start | bytes 393220
  16.5 41.7 %all-to-all-start.1 = ((s32[1,2,2048]{1,0,2:T(1,128)}), s32[1,2,2048]{1,0,2:T(1,128)S(1)}, u32[]{:S(2)}, u32[]{:S(2)}) async-start(s32[1,2,2048]{1,0,2:T(1,128)} %bitcast.7), calls=%async_computation.2 | async-start | bytes 2097152 | tf_op jit(solution)/shard_map/all_to_all | solution.py:112
  29.9 244.7 %copy-start.12 = (f32[16]{0:T(128)}, f32[16]{0:T(128)S(1)}, u32[]{:S(2)}) copy-start(f32[16]{0:T(128)S(1)} %add_add_fusion) | copy-start | bytes 196
  58.2 135.2 %all-to-all-start.2 = ((bf16[64,2,512]{2,1,0:T(2,128)(2,1)}), bf16[64,2,512]{2,1,0:T(2,128)(2,1)S(1)}, u32[]{:S(2)}, u32[]{:S(2)}) async-start(bf16[64,2,512]{2,1,0:T(2,128)(2,1)} %reshape.311), calls=%async_computation.3 | async-start | bytes 262144 | tf_op jit(solution)/shard_map/all_to_all | solution.py:111
  193.4 48.7 %all-to-all-start = ((bf16[64,2,4096]{2,1,0:T(2,128)(2,1)}), bf16[64,2,4096]{2,1,0:T(2,128)(2,1)S(1)}, u32[]{:S(2)}, u32[]{:S(2)}) async-start(bf16[64,2,4096]{2,1,0:T(2,128)(2,1)} %reshape.309), calls=%async_computation.1 | async-start | bytes 2097152 | tf_op jit(solution)/shard_map/all_to_all | solution.py:110
  217.4 13.3 %copy-start.9 = (f32[16,8,2,8]{3,1,0,2:T(8,128)S(1)}, f32[16,8,2,8]{3,1,0,2:T(8,128)}, u32[]{:S(2)}) copy-start(f32[16,8,2,8]{3,1,0,2:T(8,128)} %constant.98) | copy-start | bytes 24580
  217.4 15.6 %copy-start.20 = (f32[16,8,2,512]{3,1,2,0:T(8,128)S(1)}, f32[16,8,2,512]{3,1,2,0:T(8,128)}, u32[]{:S(2)}) copy-start(f32[16,8,2,512]{3,1,2,0:T(8,128)} %constant.89.clone.1) | copy-start | bytes 1572868
  230.6 103.8 %copy-start.16 = (s32[2048]{0:T(1024)}, s32[2048]{0:T(1024)S(1)}, u32[]{:S(2)}) copy-start(s32[2048]{0:T(1024)S(1)} %gather_fusion) | copy-start | bytes 24580
  258.9 1.6 copy-start.2
  268.3 6.3 %collective-permute-start.1 = (f32[1,16,8]{0,2,1:T(8,128)S(1)}, f32[1,16,8]{0,2,1:T(8,128)S(1)}, u32[]{:S(2)}, u32[]{:S(2)}) collective-permute-start(f32[1,16,8]{0,2,1:T(8,128)S(1)} %copy.127), channel_id=1, source_target_pairs={{1,0},{2,1},{3,2},{5,4},{6,5},{7,6},{9,8},{10,9},{11,10},{13,12},{... | collective-permute-start | bytes 1544 | tf_op jit(solution)/shard_map/ppermute | solution.py:19
  269.7 4.8 collective-permute-start
  342.3 4.0 copy-start.4
  342.3 4.0 copy-start.6
  342.3 13.2 %copy-start.13 = (f32[16]{0:T(128)S(1)}, f32[16]{0:T(128)}, u32[]{:S(2)}) copy-start(f32[16]{0:T(128)} %copy-done.12) | copy-start | bytes 196
  346.7 5.3 %collective-permute-start.2 = (f32[1,16,8]{0,2,1:T(8,128)S(1)}, f32[1,16,8]{0,2,1:T(8,128)S(1)}, u32[]{:S(2)}, u32[]{:S(2)}) collective-permute-start(f32[1,16,8]{0,2,1:T(8,128)S(1)} %copy.138), channel_id=1, source_target_pairs={{0,1},{1,2},{2,3},{4,5},{5,6},{6,7},{8,9},{9,10},{10,11},{12,13},{... | collective-permute-start | bytes 1544 | tf_op jit(solution)/shard_map/ppermute | solution.py:18
  350.6 5.0 collective-permute-start.3
  409.2 3.6 copy-start.17
  420.7 4.0 copy-start.5
  420.8 4.0 copy-start.7
  420.8 12.7 %copy-start.14 = (f32[16]{0:T(128)S(1)}, f32[16]{0:T(128)}, u32[]{:S(2)}) copy-start(f32[16]{0:T(128)} %copy-done.12) | copy-start | bytes 196
  425.1 4.8 collective-permute-start.4
  428.5 5.0 collective-permute-start.5
  487.1 3.0 copy-start.18
  495.4 15.4 %copy-start.1 = (bf16[4,64,16,256]{3,2,1,0:T(8,128)(2,1)S(1)}, bf16[4,64,16,256]{3,2,1,0:T(8,128)(2,1)}, u32[]{:S(2)}) copy-start(bf16[4,64,16,256]{3,2,1,0:T(8,128)(2,1)} %param.11) | copy-start | bytes 6291460
  497.2 12.7 %copy-start.15 = (f32[16]{0:T(128)S(1)}, f32[16]{0:T(128)}, u32[]{:S(2)}) copy-start(f32[16]{0:T(128)} %copy-done.12) | copy-start | bytes 196
  501.6 4.8 collective-permute-start.6
  504.9 5.0 collective-permute-start.7
Sparse Core Ops, SparseCore 0:
  14.6 53.0 reduce-scatter.1
where the time goes:
time: 525 us; the launch traced here: 518 us
  local copies, waits for them, and re-layouts  209 us (40%)
  blocking collectives  163 us (31%)
  starting transfers between devices  49 us (9%)
  waiting for transfers between devices  34.6 us (7%)
  matrix products  34.3 us (7%)
  between operations  14.5 us (3%)
  other arithmetic  13.8 us (3%)
    all_gather x3, blocking collectives, body(): all_gains = lax.all_gather(gain_shard, 'bl', axis=2, tiled=True)  163 us
    slice x1, local copies, waits for them, and re-layouts, body(): first_slot = inverse[packed[0, 0]]  106 us
    unnamed x55, local copies, waits for them, and re-layouts  36.5 us
    all_to_all x1, waiting for transfers between devices, body(): lax.all_to_all(packed, 'bl', split_axis=2, concat_axis=2, tiled=True)  23.2 us
    dot_general x4, matrix products, body(): jnp.einsum('fv,sv->fs', stacked, near_pick, precision=lax.Precision.HIGHE...  15.8 us
    dot_general x8, matrix products, lookup(): jnp.dot(gain_flat, pick, precision=lax.Precision.HIGHEST, preferred_eleme...  14.9 us
    ppermute x4, starting transfers between devices, extended(): before = lax.ppermute(last, axis, up)  13.8 us
    gather x1, local copies, waits for them, and re-layouts, body(): first_slot = inverse[packed[0, 0]]  13.2 us
  transfers between devices with their start and end apart: 12, of which 5 were waited for; matrix products, arithmetic and copies ran while one was open for 34% of the time, Pallas kernels for 0%

commit v1 on v0

--- a/solution.py
+++ b/solution.py
@@ -132,7 +132,12 @@
     )
     for iteration in range(ITERS):
         if iteration > 0:
-            all_gains = lax.all_gather(gain_shard, "bl", axis=2, tiled=True)
+            all_gains = jnp.concatenate(
+                lax.all_to_all(
+                    jnp.stack([gain_shard for _ in range(lax.axis_size("bl"))], axis=0), "bl", 0, 0
+                ),
+                2,
+            )
         far_gain = lookup(all_gains.reshape(channels * 2 * ND, S), far_pick)
         near_gain = lookup(gain_shard.reshape(channels * 2 * ND, owned), near_pick)
         stacked = row_terms(model_vis, visible, far_gain, near_gain)

time: 525 us -> 487 us (0.928)
  blocking collectives: 163 us -> 0 us
  local copies, waits for them, and re-layouts: 209 us -> 254 us
  waiting for transfers between devices: 34.6 us -> 78.6 us
  starting transfers between devices: 49 us -> 76.2 us
    all_gather x3 -> x0, blocking collectives: 163 us -> none  [body(): all_gains = lax.all_gather(gain_shard, 'bl', axis=2, tiled=True)]
    all_to_all x0 -> x3, waiting for transfers between devices: none -> 43.9 us  [body(): lax.all_to_all(jnp.stack([gain_shard for _ in range(lax.axis_size('bl'))]...]
    all_to_all x0 -> x3, starting transfers between devices: none -> 27.1 us  [body(): lax.all_to_all(jnp.stack([gain_shard for _ in range(lax.axis_size('bl'))]...]
    unnamed x55 -> x48, local copies, waits for them, and re-layouts: 36.5 us -> 59.8 us
    reshape x0 -> x6, local copies, waits for them, and re-layouts: none -> 14.5 us  [body(): jnp.concatenate(lax.all_to_all(jnp.stack([gain_shard for _ in range(lax.a...]
    slice x1, local copies, waits for them, and re-layouts: 106 us -> 115 us  [body(): first_slot = inverse[packed[0, 0]]]
    all_to_all x0 -> x3, other arithmetic: none -> 5.65 us  [body(): lax.all_to_all(jnp.stack([gain_shard for _ in range(lax.axis_size('bl'))]...]
  transfers between devices with their start and end apart: 12 -> 15, of which waited for: 5 -> 8; matrix products, arithmetic and copies ran while one was open for 34% -> 40% of each run, Pallas kernels for 0% -> 0%
where the time goes in v1:
time: 487 us; the launch traced here: 480 us
  local copies, waits for them, and re-layouts  254 us (52%)
  waiting for transfers between devices  78.6 us (16%)
  starting transfers between devices  76.2 us (16%)
  matrix products  38.4 us (8%)
  other arithmetic  17.7 us (4%)
  between operations  14.5 us (3%)
    slice x1, local copies, waits for them, and re-layouts, body(): first_slot = inverse[packed[0, 0]]  115 us
    unnamed x48, local copies, waits for them, and re-layouts  59.8 us
    all_to_all x3, waiting for transfers between devices, body(): lax.all_to_all(jnp.stack([gain_shard for _ in range(lax.axis_size('bl'))]...  43.9 us
    all_to_all x3, starting transfers between devices, body(): lax.all_to_all(jnp.stack([gain_shard for _ in range(lax.axis_size('bl'))]...  27.1 us
    all_to_all x1, waiting for transfers between devices, body(): lax.all_to_all(packed, 'bl', split_axis=2, concat_axis=2, tiled=True)  23.3 us
    dot_general x8, matrix products, lookup(): jnp.dot(gain_flat, pick, precision=lax.Precision.HIGHEST, preferred_eleme...  18.9 us
    dot_general x4, matrix products, body(): jnp.einsum('fv,sv->fs', stacked, near_pick, precision=lax.Precision.HIGHE...  15.8 us
    reshape x6, local copies, waits for them, and re-layouts, body(): jnp.concatenate(lax.all_to_all(jnp.stack([gain_shard for _ in range(lax.a...  14.5 us
  transfers between devices with their start and end apart: 15, of which 8 were waited for; matrix products, arithmetic and copies ran while one was open for 40% of the time, Pallas kernels for 0%

profile of v1, /device:TPU:1, one launch (start us, length us, event | category | flops | bytes accessed | tf_op | source)
XLA Modules:
  0.0 479.7 jit_solution(3743086793518295845)
XLA Ops:
  8.1 2.4 fusion.41
  11.9 2.6 copy.206
  16.6 13.1 %all-to-all-start.1 = ((s32[1,2,2048]{1,0,2:T(1,128)}), s32[1,2,2048]{1,0,2:T(1,128)S(1)}, u32[]{:S(2)}, u32[]{:S(2)}) async-start(s32[1,2,2048]{1,0,2:T(1,128)} %bitcast.7), calls=%async_computation.2 | async-start | bytes 2097152 | tf_op jit(solution)/shard_map/all_to_all | solution.py:112
  32.5 2.4 scatter_custom_fusion
  35.0 23.3 %all-to-all-done.1 = s32[1,2,2048]{1,0,2:T(1,128)S(1)} async-done(((s32[1,2,2048]{1,0,2:T(1,128)}), s32[1,2,2048]{1,0,2:T(1,128)S(1)}, u32[]{:S(2)}, u32[]{:S(2)}) %all-to-all-start.1) | async-done | bytes 16416 | tf_op jit(solution)/shard_map/all_to_all | solution.py:112
  58.3 6.2 %all-to-all-start.2 = ((bf16[64,2,512]{2,1,0:T(2,128)(2,1)}), bf16[64,2,512]{2,1,0:T(2,128)(2,1)S(1)}, u32[]{:S(2)}, u32[]{:S(2)}) async-start(bf16[64,2,512]{2,1,0:T(2,128)(2,1)} %reshape.326), calls=%async_computation.3 | async-start | bytes 262144 | tf_op jit(solution)/shard_map/all_to_all | solution.py:111
  64.5 115.0 %slice_reduce_fusion = (s32[2048]{0:T(1024)S(1)}, s32[2048]{0:T(1024)S(1)}) fusion(s32[1,2,2048]{1,0,2:T(1,128)S(1)} %all-to-all-done.1), kind=kLoop, calls=%fused_computation.86 | loop fusion | bytes 32768 | tf_op jit(solution)/shard_map/slice | solution.py:114
  181.1 8.6 %copy.107 = bf16[16,16,2048]{1,0,2:T(8,128)(2,1)} copy(bf16[16,16,2048]{2,1,0:T(8,128)(2,1)S(1)} %multiply_convert_fusion) | data formatting | bytes 2097152 | tf_op jit(solution)/shard_map/convert_element_type | solution.py:102
  189.6 12.5 %reshape.324 = bf16[64,2,4096]{2,1,0:T(2,128)(2,1)} reshape(bf16[2048,16,16]{2,1,0:T(8,128)(2,1)} %bitcast.265) | data formatting | bytes 2097152
  202.1 10.6 %all-to-all-start = ((bf16[64,2,4096]{2,1,0:T(2,128)(2,1)}), bf16[64,2,4096]{2,1,0:T(2,128)(2,1)S(1)}, u32[]{:S(2)}, u32[]{:S(2)}) async-start(bf16[64,2,4096]{2,1,0:T(2,128)(2,1)} %reshape.324), calls=%async_computation.1 | async-start | bytes 2097152 | tf_op jit(solution)/shard_map/all_to_all | solution.py:110
  212.7 13.2 %gather_fusion.1 = s32[2048]{0:T(1024)S(1)} fusion(s32[512]{0:T(512)S(1)} %scatter_custom_fusion, s32[2048]{0:T(1024)S(1)} %broadcast_clamp_fusion), kind=kCustom, calls=%fused_computation.1 | custom fusion | bytes 24576 | tf_op jit(solution)/shard_map/gather | solution.py:114
  226.0 13.2 %gather_fusion = s32[2048]{0:T(1024)S(1)} fusion(s32[512]{0:T(512)S(1)} %scatter_custom_fusion, s32[2048]{0:T(1024)S(1)} %broadcast_clamp_fusion.1), kind=kCustom, calls=%fused_computation | custom fusion | bytes 24576 | tf_op jit(solution)/shard_map/gather | solution.py:115
  241.6 3.4 fusion.8
  250.7 7.6 %reshape.325 = bf16[2048,16,16]{2,1,0:T(8,128)(2,1)} reshape(bf16[64,2,4096]{2,1,0:T(2,128)(2,1)S(1)} %all-to-all-done) | data formatting | bytes 2097152
  258.3 9.1 %copy.108 = bf16[16,16,2048]{2,0,1:T(8,128)(2,1)S(1)} copy(bf16[16,16,2048]{1,0,2:T(8,128)(2,1)} %bitcast.266) | data formatting | bytes 2097152 | tf_op jit(solution)/shard_map/all_to_all | solution.py:110
  269.0 2.9 subtract_reduce_fusion.3
  272.5 3.9 fusion.10
  278.2 4.0 collective-permute-start
  283.3 2.5 broadcast_bitcast_fusion.2
  285.7 4.6 reshape.328
  290.3 11.5 %all-to-all-start.3 = ((f32[64,1,2048]{2,1,0:T(1,128)}), f32[64,1,2048]{2,1,0:T(1,128)S(1)}, u32[]{:S(2)}, u32[]{:S(2)}) async-start(f32[64,1,2048]{2,1,0:T(1,128)} %reshape.328), calls=%async_computation.4 | async-start | bytes 1048576 | tf_op jit(solution)/shard_map/all_to_all | solution.py:136
  304.4 14.6 %all-to-all-done.3 = f32[64,1,2048]{2,1,0:T(1,128)S(1)} async-done(((f32[64,1,2048]{2,1,0:T(1,128)}), f32[64,1,2048]{2,1,0:T(1,128)S(1)}, u32[]{:S(2)}, u32[]{:S(2)}) %all-to-all-start.3) | async-done | bytes 524320 | tf_op jit(solution)/shard_map/all_to_all | solution.py:136
  321.5 2.8 reshape.329
  324.3 2.5 bitcast_bitcast_fusion.2
  329.1 2.9 copy.176
  336.0 3.9 fusion.16
  340.4 3.9 collective-permute-start.2
  346.0 3.6 collective-permute-done.3
  349.7 2.5 broadcast_bitcast_fusion.1
  352.2 4.2 reshape.330
  356.4 8.0 %all-to-all-start.4 = ((f32[64,1,2048]{2,1,0:T(1,128)}), f32[64,1,2048]{2,1,0:T(1,128)S(1)}, u32[]{:S(2)}, u32[]{:S(2)}) async-start(f32[64,1,2048]{2,1,0:T(1,128)} %reshape.330), calls=%async_computation.5 | async-start | bytes 1048576 | tf_op jit(solution)/shard_map/all_to_all | solution.py:136
  367.0 14.6 %all-to-all-done.4 = f32[64,1,2048]{2,1,0:T(1,128)S(1)} async-done(((f32[64,1,2048]{2,1,0:T(1,128)}), f32[64,1,2048]{2,1,0:T(1,128)S(1)}, u32[]{:S(2)}, u32[]{:S(2)}) %all-to-all-start.4) | async-done | bytes 524320 | tf_op jit(solution)/shard_map/all_to_all | solution.py:136
  383.5 2.8 reshape.331
  386.3 2.5 bitcast_bitcast_fusion.1
  391.2 2.9 copy.180
  398.1 3.9 fusion.22
  402.4 3.1 collective-permute-start.4
  407.2 3.6 collective-permute-done.5
  410.9 2.5 broadcast_bitcast_fusion
  413.4 4.2 reshape.332
  417.6 7.6 %all-to-all-start.5 = ((f32[64,1,2048]{2,1,0:T(1,128)}), f32[64,1,2048]{2,1,0:T(1,128)S(1)}, u32[]{:S(2)}, u32[]{:S(2)}) async-start(f32[64,1,2048]{2,1,0:T(1,128)} %reshape.332), calls=%async_computation.6 | async-start | bytes 1048576 | tf_op jit(solution)/shard_map/all_to_all | solution.py:136
  427.9 14.6 %all-to-all-done.5 = f32[64,1,2048]{2,1,0:T(1,128)S(1)} async-done(((f32[64,1,2048]{2,1,0:T(1,128)}), f32[64,1,2048]{2,1,0:T(1,128)S(1)}, u32[]{:S(2)}, u32[]{:S(2)}) %all-to-all-start.5) | async-done | bytes 524320 | tf_op jit(solution)/shard_map/all_to_all | solution.py:136
  444.4 2.8 reshape.333
  447.2 2.5 bitcast_bitcast_fusion
  452.0 2.9 copy.184
  459.0 3.9 fusion.28
  463.4 3.1 collective-permute-start.6
  468.2 3.6 collective-permute-done.7
  (138 shorter events, 62.6 us)
Async XLA Ops:
  6.5 1.6 copy-start
  6.5 4.0 copy-start.6
  6.5 173.0 %reduce-scatter.2.cloned.1.call-start = ((), (), s32[]{:S(2)}) async-start(), calls=%async_computation.7 | async-start | bytes 5242880 | tf_op jit(solution)/shard_map/reduce_scatter | solution.py:93
  14.5 0.7 copy-start.10
  14.5 15.3 %copy-start.11 = (s32[512]{0:T(512)S(1)}, s32[512]{0:T(512)}, u32[]{:S(2)}) copy-start(s32[512]{0:T(512)} %param.17) | copy-start | bytes 6148
  14.5 15.3 %copy-start.9 = (s32[16,2048]{1,0:T(8,128)S(1)}, s32[16,2048]{1,0:T(8,128)}, u32[]{:S(2)}) copy-start(s32[16,2048]{1,0:T(8,128)} %param.15) | copy-start | bytes 393220
  14.5 15.3 %copy-start.7 = (bf16[16,2,2048]{2,1,0:T(2,128)(2,1)S(1)}, bf16[16,2,2048]{2,1,0:T(2,128)(2,1)}, u32[]{:S(2)}) copy-start(bf16[16,2,2048]{2,1,0:T(2,128)(2,1)} %param.14) | copy-start | bytes 393220
  16.6 41.7 %all-to-all-start.1 = ((s32[1,2,2048]{1,0,2:T(1,128)}), s32[1,2,2048]{1,0,2:T(1,128)S(1)}, u32[]{:S(2)}, u32[]{:S(2)}) async-start(s32[1,2,2048]{1,0,2:T(1,128)} %bitcast.7), calls=%async_computation.2 | async-start | bytes 2097152 | tf_op jit(solution)/shard_map/all_to_all | solution.py:112
  58.3 143.8 %all-to-all-start.2 = ((bf16[64,2,512]{2,1,0:T(2,128)(2,1)}), bf16[64,2,512]{2,1,0:T(2,128)(2,1)S(1)}, u32[]{:S(2)}, u32[]{:S(2)}) async-start(bf16[64,2,512]{2,1,0:T(2,128)(2,1)} %reshape.326), calls=%async_computation.3 | async-start | bytes 262144 | tf_op jit(solution)/shard_map/all_to_all | solution.py:111
  202.1 48.6 %all-to-all-start = ((bf16[64,2,4096]{2,1,0:T(2,128)(2,1)}), bf16[64,2,4096]{2,1,0:T(2,128)(2,1)S(1)}, u32[]{:S(2)}, u32[]{:S(2)}) async-start(bf16[64,2,4096]{2,1,0:T(2,128)(2,1)} %reshape.324), calls=%async_computation.1 | async-start | bytes 2097152 | tf_op jit(solution)/shard_map/all_to_all | solution.py:110
  226.0 13.3 %copy-start.8 = (f32[16,8,2,8]{3,1,0,2:T(8,128)S(1)}, f32[16,8,2,8]{3,1,0,2:T(8,128)}, u32[]{:S(2)}) copy-start(f32[16,8,2,8]{3,1,0,2:T(8,128)} %constant.98) | copy-start | bytes 24580
  226.0 15.6 %copy-start.12 = (f32[16,8,2,512]{3,1,2,0:T(8,128)S(1)}, f32[16,8,2,512]{3,1,2,0:T(8,128)}, u32[]{:S(2)}) copy-start(f32[16,8,2,512]{3,1,2,0:T(8,128)} %constant.89.clone.1) | copy-start | bytes 1572868
  267.4 1.6 copy-start.2
  276.8 6.3 %collective-permute-start.1 = (f32[1,16,8]{0,2,1:T(8,128)S(1)}, f32[1,16,8]{0,2,1:T(8,128)S(1)}, u32[]{:S(2)}, u32[]{:S(2)}) collective-permute-start(f32[1,16,8]{0,2,1:T(8,128)S(1)} %copy.127), channel_id=1, source_target_pairs={{1,0},{2,1},{3,2},{5,4},{6,5},{7,6},{9,8},{10,9},{11,10},{13,12},{... | collective-permute-start | bytes 1544 | tf_op jit(solution)/shard_map/ppermute | solution.py:19
  278.2 4.8 collective-permute-start
  290.3 28.8 %all-to-all-start.3 = ((f32[64,1,2048]{2,1,0:T(1,128)}), f32[64,1,2048]{2,1,0:T(1,128)S(1)}, u32[]{:S(2)}, u32[]{:S(2)}) async-start(f32[64,1,2048]{2,1,0:T(1,128)} %reshape.328), calls=%async_computation.4 | async-start | bytes 1048576 | tf_op jit(solution)/shard_map/all_to_all | solution.py:136
  332.0 2.1 copy-start.4
  340.4 5.6 %collective-permute-start.2 = (f32[1,16,8]{0,2,1:T(8,128)S(1)}, f32[1,16,8]{0,2,1:T(8,128)S(1)}, u32[]{:S(2)}, u32[]{:S(2)}) collective-permute-start(f32[1,16,8]{0,2,1:T(8,128)S(1)} %copy.138), channel_id=1, source_target_pairs={{0,1},{1,2},{2,3},{4,5},{5,6},{6,7},{8,9},{9,10},{10,11},{12,13},{... | collective-permute-start | bytes 1544 | tf_op jit(solution)/shard_map/ppermute | solution.py:18
  344.6 5.0 %collective-permute-start.3 = (f32[1,16,8]{0,2,1:T(8,128)S(1)}, f32[1,16,8]{0,2,1:T(8,128)S(1)}, u32[]{:S(2)}, u32[]{:S(2)}) collective-permute-start(f32[1,16,8]{0,2,1:T(8,128)S(1)} %copy.141), channel_id=1, source_target_pairs={{1,0},{2,1},{3,2},{5,4},{6,5},{7,6},{9,8},{10,9},{11,10},{13,12},{... | collective-permute-start | bytes 1544 | tf_op jit(solution)/shard_map/ppermute | solution.py:19
  356.4 25.3 %all-to-all-start.4 = ((f32[64,1,2048]{2,1,0:T(1,128)}), f32[64,1,2048]{2,1,0:T(1,128)S(1)}, u32[]{:S(2)}, u32[]{:S(2)}) async-start(f32[64,1,2048]{2,1,0:T(1,128)} %reshape.330), calls=%async_computation.5 | async-start | bytes 1048576 | tf_op jit(solution)/shard_map/all_to_all | solution.py:136
  394.1 2.1 copy-start.5
  402.4 4.8 collective-permute-start.4
  405.8 5.0 %collective-permute-start.5 = (f32[1,16,8]{0,2,1:T(8,128)S(1)}, f32[1,16,8]{0,2,1:T(8,128)S(1)}, u32[]{:S(2)}, u32[]{:S(2)}) collective-permute-start(f32[1,16,8]{0,2,1:T(8,128)S(1)} %copy.155), channel_id=1, source_target_pairs={{1,0},{2,1},{3,2},{5,4},{6,5},{7,6},{9,8},{10,9},{11,10},{13,12},{... | collective-permute-start | bytes 1544 | tf_op jit(solution)/shard_map/ppermute | solution.py:19
  417.6 24.9 %all-to-all-start.5 = ((f32[64,1,2048]{2,1,0:T(1,128)}), f32[64,1,2048]{2,1,0:T(1,128)S(1)}, u32[]{:S(2)}, u32[]{:S(2)}) async-start(f32[64,1,2048]{2,1,0:T(1,128)} %reshape.332), calls=%async_computation.6 | async-start | bytes 1048576 | tf_op jit(solution)/shard_map/all_to_all | solution.py:136
  454.9 2.1 copy-start.3
  458.5 14.1 %copy-start.1 = (bf16[4,64,16,256]{3,2,1,0:T(8,128)(2,1)S(1)}, bf16[4,64,16,256]{3,2,1,0:T(8,128)(2,1)}, u32[]{:S(2)}) copy-start(bf16[4,64,16,256]{3,2,1,0:T(8,128)(2,1)} %param.11) | copy-start | bytes 6291460
  463.4 4.8 %collective-permute-start.6 = (f32[1,16,8]{0,2,1:T(8,128)S(1)}, f32[1,16,8]{0,2,1:T(8,128)S(1)}, u32[]{:S(2)}, u32[]{:S(2)}) collective-permute-start(f32[1,16,8]{0,2,1:T(8,128)S(1)} %copy.166), channel_id=1, source_target_pairs={{0,1},{1,2},{2,3},{4,5},{5,6},{6,7},{8,9},{9,10},{10,11},{12,13},{... | collective-permute-start | bytes 1544 | tf_op jit(solution)/shard_map/ppermute | solution.py:18
  466.7 5.0 %collective-permute-start.7 = (f32[1,16,8]{0,2,1:T(8,128)S(1)}, f32[1,16,8]{0,2,1:T(8,128)S(1)}, u32[]{:S(2)}, u32[]{:S(2)}) collective-permute-start(f32[1,16,8]{0,2,1:T(8,128)S(1)} %copy.169), channel_id=1, source_target_pairs={{1,0},{2,1},{3,2},{5,4},{6,5},{7,6},{9,8},{10,9},{11,10},{13,12},{... | collective-permute-start | bytes 1544 | tf_op jit(solution)/shard_map/ppermute | solution.py:19
Sparse Core Ops, SparseCore 0:
  14.6 53.0 reduce-scatter.1
